TPU v7x, 32 devices: a whole 2x2x4 slice. The times are simulated.
32 devices in a mesh: groups: 2 (over y), tiles: 4 (over z), folds: 2 (over x), sub: 2 (over core).
Axes of the slice: x: 2, y: 2, z: 4, core: 2. Of those that a mesh axis runs over, the one named last changes fastest.
Arguments:
- features: bfloat16 [2, 32, 16, 16, 1024], P('folds', ('groups', 'tiles', 'sub')), parts along dimension 1, may hold values from -6 to 6
- conv_first: bfloat16 [2, 3, 3, 3, 64, 32], P('folds'), may hold values from -0.15625 to 0.15625
- gain_first: float32 [2, 32], P('folds'), may hold values from 0.1 to 1.9
- shift_first: float32 [2, 32], P('folds'), may hold values from -3 to 3
- conv_second: bfloat16 [2, 3, 3, 3, 32, 32], P('folds'), may hold values from -0.21875 to 0.21875
- gain_second: float32 [2, 32], P('folds'), may hold values from 0.1 to 1.9
- shift_second: float32 [2, 32], P('folds'), may hold values from -3 to 3
- head_weight: bfloat16 [2, 32, 16], P('folds'), may hold values from -1 to 1
- head_bias: float32 [2, 16], P('folds'), may hold values from -4 to 4
- corners: int32 [32, 3], P(('groups', 'tiles', 'sub')), parts along dimension 0, may hold values from 0 to 48, as said below
- counts: int32 [8, 2], P('groups'), parts along dimension 0, may hold values from 0 to 2, as said below
Outputs:
- logits: float32 [128, 40, 640], P(('groups', 'tiles'), ('folds', 'sub')), parts along dimension 0
There are 2 independent parts, one for each index of `groups`. A program takes and returns all parts, laid end to end along the dimension named above; an argument that names none is the same for every part. Nothing has to cross between parts.
Inputs may be any that keep to these rules, and one draw needn't show every extreme that they name: `corners`: for slot n = (t * 2 + s) * 2 + j, the z coordinate lies in [t * 16, (t + 1) * 16) and equals (3) * 16 in the last slab; x lies in [0, 24] and y in [0, 24]. counts[t, s] + counts[t xor (2), s] <= 2 for every t and s; some entry equals 2.
All inputs are finite; a program needn't handle non-finite values.
Results may differ from a plain program's by a relative error of at most 0.01.
Values may be sent and summed in bfloat16 or wider, within the bound.
A program may use at most 128 MiB of HBM per device.

v0:
```python
import functools

import jax
import jax.numpy as jnp
from jax import lax
from jax.experimental import pallas as pl
from jax.experimental.pallas import tpu as pltpu
from jax.sharding import PartitionSpec as P

CH = 32
CLASSES = 16
WE = 16
TZ = 16
VX = 40
VY = 40
ROWS = WE * WE
EXT = TZ + WE
LANES = WE * CLASSES + 128

epsilon = 1e-05
leak_slope = 0.01

f32 = jnp.float32
bf16 = jnp.bfloat16


def iota(shape, dim):
    return lax.broadcasted_iota(jnp.int32, shape, dim)


def one_hot(mask):
    return jnp.where(mask, 1.0, 0.0)


def exact_dot(a, b):
    return jnp.dot(a, b, precision=lax.Precision.HIGHEST, preferred_element_type=f32)


def spread_lanes(vec, width):
    n = vec.shape[1]
    pick = one_hot(iota((n, width), 0) == iota((n, width), 1) % n)
    return exact_dot(vec, pick)


def build_band(taps_ref, band, in_width, lead):
    pick = one_hot(iota((CH, 8 * CH), 0) == iota((CH, 8 * CH), 1) % CH).astype(bf16)
    band[...] = jnp.zeros_like(band)
    out_voxel = iota((in_width, 8 * CH), 1) // CH
    for dz in range(3):
        for dx in range(3):
            start = (dz * 3 + dx) * 3 * in_width
            spread = [
                jnp.dot(
                    taps_ref[start + dy * in_width : start + (dy + 1) * in_width, :],
                    pick,
                    preferred_element_type=f32,
                )
                for dy in range(3)
            ]
            for r in range(-1, 9):
                block = jnp.zeros((in_width, 8 * CH), f32)
                for dy in range(3):
                    if 0 <= r + 1 - dy < 8:
                        block = jnp.where(out_voxel == r + 1 - dy, spread[dy], block)
                band[
                    dz,
                    (r + lead) * in_width : (r + lead + 1) * in_width,
                    dx * 8 * CH : (dx + 1) * 8 * CH,
                ] = block.astype(bf16)


def convolve(padded, band, hidden, columns, band_rows):
    n = padded.shape[0]
    across = iota((n * ROWS, 8 * CH), 0) % WE
    for block in range(2):
        lo, width = columns[block]
        view = jnp.concatenate(
            [
                jnp.concatenate(
                    [padded[w, dz * WE : dz * WE + ROWS, lo : lo + width] for dz in range(3)],
                    axis=1,
                )
                for w in range(n)
            ],
            axis=0,
        )
        first = band_rows[block]
        weights = jnp.concatenate([band[dz, first : first + width, :] for dz in range(3)], axis=0)
        res = jnp.dot(view, weights, preferred_element_type=f32)
        before = pltpu.roll(res[:, : 8 * CH], 1, 0)
        after = pltpu.roll(res[:, 16 * CH :], n * ROWS - 1, 0)
        hidden[:, block * 8 * CH : (block + 1) * 8 * CH] = (
            res[:, 8 * CH : 16 * CH]
            + jnp.where(across == 0, 0.0, before)
            + jnp.where(across == WE - 1, 0.0, after)
        )


def group_sum(row):
    by = row.shape[1] // 2
    while by >= CH:
        row = row + pltpu.roll(row, by, 1)
        by //= 2
    return row


def normalize(hidden, gain, shift):
    voxels = float(WE * WE * WE)
    mean_value = group_sum(jnp.sum(hidden, axis=0, keepdims=True)) / voxels
    centered = hidden - mean_value
    variance = group_sum(jnp.sum(centered * centered, axis=0, keepdims=True)) / voxels
    scaled = centered * (lax.rsqrt(variance + epsilon) * gain) + shift
    return jnp.where(scaled >= 0, scaled, leak_slope * scaled).astype(bf16)


def decode_kernel(
    features,
    taps_first,
    gain_first,
    shift_first,
    taps_second,
    gain_second,
    shift_second,
    head_weight,
    head_bias,
    corners,
    counts,
    out,
    padded,
    normed,
    band_first,
    band_second,
    hidden,
    ext,
    sems,
):
    n = padded.shape[0]
    cin = padded.shape[2] // WE
    loads = [
        pltpu.make_async_copy(features.at[w], padded.at[w, WE : WE + ROWS, :], sems.at[w])
        for w in range(n)
    ]
    for load in loads:
        load.start()
    for w in range(n):
        padded[w, :WE, :] = jnp.zeros((WE, padded.shape[2]), bf16)
        padded[w, WE + ROWS :, :] = jnp.zeros((WE, padded.shape[2]), bf16)
        normed[w, :WE, :] = jnp.zeros((WE, normed.shape[2]), bf16)
        normed[w, WE + ROWS :, :] = jnp.zeros((WE, normed.shape[2]), bf16)
    ext[...] = jnp.zeros_like(ext)
    build_band(taps_first, band_first, cin, 4)
    build_band(taps_second, band_second, CH, 8)
    gains = [spread_lanes(g[...], WE * CH) for g in (gain_first, gain_second)]
    shifts = [spread_lanes(s[...], WE * CH) for s in (shift_first, shift_second)]
    for load in loads:
        load.wait()
    convolve(padded, band_first, hidden, ((0, 12 * cin), (4 * cin, 12 * cin)), (4 * cin, 0))
    for w in range(n):
        normed[w, WE : WE + ROWS, :] = normalize(
            hidden[w * ROWS : (w + 1) * ROWS, :], gains[0], shifts[0]
        )
    convolve(normed, band_second, hidden, ((0, 16 * CH), (0, 16 * CH)), (8 * CH, 0))

    tile = lax.axis_index("tiles")
    live_count = counts[tile, lax.axis_index("sub")]
    width = WE * CH
    pick_rows = one_hot(iota((width, CH), 0) % CH == iota((width, CH), 1)).astype(bf16)
    pick_lanes = one_hot(iota((CLASSES, LANES), 0) == iota((CLASSES, LANES), 1) % CLASSES)
    head_rows = jnp.dot(pick_rows, head_weight[...], preferred_element_type=f32).astype(bf16)
    head_full = jnp.dot(head_rows, pick_lanes.astype(bf16), preferred_element_type=f32)
    bias = spread_lanes(head_bias[...], LANES)
    head_gap = iota((width, LANES), 1) // CLASSES - iota((width, LANES), 0) // CH
    place_rows = iota((WE * EXT, ROWS), 0)
    place_cols = iota((WE * EXT, ROWS), 1)
    same_across = place_rows // EXT == place_cols % WE
    depth_gap = place_rows % EXT - place_cols // WE
    row_id = iota((WE * EXT, 1), 0)
    lane_id = iota((1, LANES), 1)
    center = (WE - 1) / 2.0
    spread = 2.0 * (WE / 4.0) ** 2
    for w in range(n):
        second = normalize(hidden[w * ROWS : (w + 1) * ROWS, :], gains[1], shifts[1])
        cz = corners[w, 0] - tile * TZ
        cx = corners[w, 1]
        cy = corners[w, 2]
        lane_tile = jnp.minimum(cy // 8, (VY - 24) // 8)
        rot = cy - lane_tile * 8
        placed = one_hot(same_across & (depth_gap == cz)).astype(bf16)
        moved = jnp.dot(placed, second, preferred_element_type=f32).astype(bf16)
        head = jnp.where(head_gap == rot, head_full, 0.0).astype(bf16)
        logits = jnp.dot(moved, head, preferred_element_type=f32) + bias
        z = row_id % EXT - cz
        across = (row_id // EXT).astype(f32) - center
        depth = z.astype(f32) - center
        gauss_rows = jnp.exp(-(depth * depth) / spread) * jnp.exp(-(across * across) / spread)
        gauss_rows = jnp.where((z >= 0) & (z < WE) & (w < live_count), gauss_rows, 0.0)
        y = lane_id // CLASSES - rot
        along = y.astype(f32) - center
        gauss_lanes = jnp.exp(-(along * along) / spread)
        gauss_lanes = jnp.where((y >= 0) & (y < WE), gauss_lanes, 0.0)
        weighted = (logits * (gauss_rows * gauss_lanes)).astype(bf16).astype(f32)
        lanes = pl.ds(pl.multiple_of(lane_tile * 128, 128), LANES)
        ext[pl.ds(cx, WE), :, lanes] += weighted.reshape(WE, EXT, LANES)
    out[...] = ext[...].astype(bf16)


def decode(features, taps_first, gf, sf, taps_second, gs, ss, hw, hb, corners, counts):
    n = features.shape[0]
    in_width = features.shape[-1]
    cin = in_width // WE
    vmem = pl.BlockSpec(memory_space=pltpu.VMEM)
    smem = pl.BlockSpec(memory_space=pltpu.SMEM)
    return pl.pallas_call(
        decode_kernel,
        out_shape=jax.ShapeDtypeStruct((VX, EXT, VY * CLASSES), bf16),
        in_specs=[pl.BlockSpec(memory_space=pl.ANY)] + [vmem] * 8 + [smem] * 2,
        out_specs=vmem,
        scratch_shapes=[
            pltpu.VMEM((n, ROWS + 2 * WE, in_width), bf16),
            pltpu.VMEM((n, ROWS + 2 * WE, WE * CH), bf16),
            pltpu.VMEM((3, 16 * cin, 24 * CH), bf16),
            pltpu.VMEM((3, 24 * CH, 24 * CH), bf16),
            pltpu.VMEM((n * ROWS, WE * CH), f32),
            pltpu.VMEM((VX, EXT, VY * CLASSES), f32),
            pltpu.SemaphoreType.DMA((n,)),
        ],
        compiler_params=pltpu.CompilerParams(vmem_limit_bytes=56 * 1024 * 1024),
    )(
        features.reshape(n, ROWS, in_width),
        taps_first.reshape(27 * cin, CH),
        gf,
        sf,
        taps_second.reshape(27 * CH, CH),
        gs,
        ss,
        hw,
        hb,
        corners,
        counts,
    )


def on_device(
    features,
    conv_first,
    gain_first,
    shift_first,
    conv_second,
    gain_second,
    shift_second,
    head_weight,
    head_bias,
    corners,
    counts,
):
    extended = decode(
        features[0],
        conv_first[0],
        gain_first,
        shift_first,
        conv_second[0],
        gain_second,
        shift_second,
        head_weight[0],
        head_bias,
        corners,
        counts,
    )
    shares = lax.psum_scatter(extended, ("folds", "sub"), scatter_dimension=0, tiled=True)
    length = lax.axis_size("tiles")
    pairs = [(i, i + 1) for i in range(length - 1)]
    arrived = lax.ppermute(shares[:, TZ:], "tiles", pairs)
    total = shares[:, :TZ].astype(f32) + arrived.astype(f32)
    return total.transpose(1, 0, 2)


def solution(mesh):
    placed = (
        P("folds", ("groups", "tiles", "sub"), None, None, None),
        P("folds", None, None, None, None, None),
        P("folds", None),
        P("folds", None),
        P("folds", None, None, None, None, None),
        P("folds", None),
        P("folds", None),
        P("folds", None, None),
        P("folds", None),
        P(("groups", "tiles", "sub"), None),
        P("groups", None),
    )
    return jax.shard_map(
        on_device,
        mesh=mesh,
        in_specs=placed,
        out_specs=P(("groups", "tiles"), ("folds", "sub"), None),
        check_vma=False,
    )
```

profile of v0, /device:TPU:0, one launch (start us, length us, event | category | flops | bytes accessed | tf_op | source)
XLA Modules:
  0.0 72.0 jit_solution(14417045815821620801)
XLA Ops:
  6.5 0.0 reduce-scatter.2.cloned.1.call-start
  6.5 1.3 %copy.14.counts = s32[4,2]{1,0:T(4,128)} copy(s32[4,2]{0,1:T(2,128)} %param.21) | data formatting | bytes 64 | tf_op args[10]
  7.9 1.4 %copy.13 = bf16[1,32,16]{2,1,0:T(8,128)(2,1)} copy(bf16[1,32,16]{1,2,0:T(8,128)(2,1)} %param.18) | data formatting | bytes 2048 | tf_op args[7]
  9.2 1.9 %copy.12 = bf16[1,3,3,3,64,32]{5,4,3,2,1,0:T(8,128)(2,1)} copy(bf16[1,3,3,3,64,32]{4,5,3,2,1,0:T(8,128)(2,1)} %param.12) | data formatting | bytes 221184 | tf_op args[1]
  11.1 12.5 %shard_map.109 = bf16[40,32,640]{2,1,0:T(8,128)(2,1)} custom-call(bf16[2,256,1024]{2,1,0:T(8,128)(2,1)} %bitcast.7, bf16[1728,32]{1,0:T(8,128)(2,1)} %bitcast.6, f32[1,32]{1,0:T(1,128)} %gain_first.1, f32[1,32]{1,0:T(1,128)} %shift_first.1, bf16[864,32]{1,0:T(8,128)(2,1)} %bitcast.8, f32[1,32]{1,0:T(1,128)} %gain_second.1, f32[1,32]{1,0:T(1,128)} %shift_second.1, ...), custom_call_target="tpu_custom_call" | custom-call | tf_op jit(solution)/shard_map/pallas_call | solution.py:213
  23.7 0.0 reduce-scatter.2.cloned.1.call-update
  23.7 31.2 %reduce-scatter.2.cloned.1.call-done = bf16[10,32,640]{2,1,0:T(8,128)(2,1)} async-done(((bf16[40,32,640]{2,1,0:T(8,128)(2,1)}), bf16[10,32,640]{2,1,0:T(8,128)(2,1)}) %reduce-scatter.2.cloned.1.call-update) | async-done | bytes 409616 | tf_op jit(solution)/shard_map/reduce_scatter | solution.py:269
  54.9 0.9 %slice.9 = bf16[10,16,640]{2,1,0:T(8,128)(2,1)S(1)} slice(bf16[10,32,640]{2,1,0:T(8,128)(2,1)} %reduce-scatter.2.cloned.1.call-done), slice={[0:10], [16:32], [0:640]} | slice | bytes 409600 | tf_op jit(solution)/shard_map/slice | solution.py:272
  55.9 3.4 %collective-permute-start = (bf16[10,16,640]{2,1,0:T(8,128)(2,1)S(1)}, bf16[10,16,640]{2,1,0:T(8,128)(2,1)S(1)}, u32[]{:S(2)}, u32[]{:S(2)}) collective-permute-start(bf16[10,16,640]{2,1,0:T(8,128)(2,1)S(1)} %slice.9), channel_id=1, source_target_pairs={{0,4},{4,8},{8,12},{1,5},{5,9},{9,13},{2,6},{6,10},{10,14},{3,7},{... | collective-permute-start | bytes 614408 | tf_op jit(solution)/shard_map/ppermute | solution.py:272
  59.3 4.1 %collective-permute-done = bf16[10,16,640]{2,1,0:T(8,128)(2,1)S(1)} collective-permute-done((bf16[10,16,640]{2,1,0:T(8,128)(2,1)S(1)}, bf16[10,16,640]{2,1,0:T(8,128)(2,1)S(1)}, u32[]{:S(2)}, u32[]{:S(2)}) %collective-permute-start) | collective-permute-done | bytes 204832 | tf_op jit(solution)/shard_map/ppermute | solution.py:272
  63.4 1.7 %add_bitcast_fusion = f32[16,10,640]{2,0,1:T(8,128)} fusion(bf16[10,16,640]{2,1,0:T(8,128)(2,1)S(1)} %collective-permute-done, bf16[10,32,640]{2,1,0:T(8,128)(2,1)} %reduce-scatter.2.cloned.1.call-done), kind=kLoop, calls=%fused_computation | loop fusion | flops 307200 | bytes 819200 | tf_op jit(solution)/shard_map/transpose | solution.py:274
Async XLA Ops:
  6.5 48.4 %reduce-scatter.2.cloned.1.call-start = ((), (), s32[]{:S(2)}) async-start(), calls=%async_computation.1 | async-start | bytes 2048000 | tf_op jit(solution)/shard_map/reduce_scatter | solution.py:269
  55.9 7.6 %collective-permute-start = (bf16[10,16,640]{2,1,0:T(8,128)(2,1)S(1)}, bf16[10,16,640]{2,1,0:T(8,128)(2,1)S(1)}, u32[]{:S(2)}, u32[]{:S(2)}) collective-permute-start(bf16[10,16,640]{2,1,0:T(8,128)(2,1)S(1)} %slice.9), channel_id=1, source_target_pairs={{0,4},{4,8},{8,12},{1,5},{5,9},{9,13},{2,6},{6,10},{10,14},{3,7},{... | collective-permute-start | bytes 614408 | tf_op jit(solution)/shard_map/ppermute | solution.py:272
Sparse Core Ops, SparseCore 0:
  23.8 31.0 reduce-scatter.1
where the time goes:
time: 72.3 us; the launch traced here: 72 us
  waiting for transfers between devices  35.4 us (49%)
  between operations  13.4 us (19%)
  Pallas kernels  12.5 us (17%)
  local copies, waits for them, and re-layouts  5.54 us (8%)
  starting transfers between devices  3.43 us (5%)
  other arithmetic  1.74 us (2%)
    reduce_scatter x1, waiting for transfers between devices, on_device(): lax.psum_scatter(extended, ('folds', 'sub'), scatter_dimension=0, tiled=T...  31.2 us
    pallas_call x1, Pallas kernels, decode(): pl.pallas_call(decode_kernel, out_shape=jax.ShapeDtypeStruct((VX, EXT, VY...  12.5 us
    unnamed x3, local copies, waits for them, and re-layouts  4.59 us
    ppermute x1, waiting for transfers between devices, on_device(): arrived = lax.ppermute(shares[:, TZ:], 'tiles', pairs)  4.13 us
    ppermute x1, starting transfers between devices, on_device(): arrived = lax.ppermute(shares[:, TZ:], 'tiles', pairs)  3.42 us
    transpose x1, other arithmetic, on_device(): return total.transpose(1, 0, 2)  1.74 us
  transfers between devices with their start and end apart: 2, of which 2 were waited for; matrix products, arithmetic and copies ran while one was open for 0% of the time, Pallas kernels for 0%

commit v1 on v0

--- a/solution.py
+++ b/solution.py
@@ -240,6 +240,179 @@
     )
 
 
+def exchange_kernel(
+    ext,
+    out,
+    got_sub,
+    part,
+    got_fold,
+    tail,
+    got_tail,
+    sub_send,
+    sub_recv,
+    fold_send,
+    fold_recv,
+    tile_send,
+    tile_recv,
+):
+    fold, sub, tile = (lax.axis_index(a) for a in ("folds", "sub", "tiles"))
+    folds, subs, tiles = (lax.axis_size(a) for a in ("folds", "sub", "tiles"))
+    span = out.shape[0]
+    chunks = 2 if span % 2 == 0 else 1
+    step = span // chunks
+    mesh_id = pl.DeviceIdType.MESH
+    barrier = pltpu.get_barrier_semaphore()
+
+    def greet(where):
+        pl.semaphore_signal(barrier, inc=1, device_id=where, device_id_type=mesh_id)
+
+    for e in range(1, subs):
+        greet({"sub": lax.rem(sub + e, subs)})
+    for d in range(1, folds):
+        greet({"folds": lax.rem(fold + d, folds)})
+
+    @pl.when(tile < tiles - 1)
+    def _():
+        greet({"tiles": tile + 1})
+
+    @pl.when(tile > 0)
+    def _():
+        greet({"tiles": tile - 1})
+
+    peers = subs - 1 + folds - 1
+    at_end = (tile == 0) | (tile == tiles - 1)
+
+    @pl.when(at_end)
+    def _():
+        pl.semaphore_wait(barrier, peers + 1)
+
+    @pl.when(jnp.logical_not(at_end))
+    def _():
+        pl.semaphore_wait(barrier, peers + 2)
+
+    def own(d, of_sub, half, k):
+        first = (lax.rem(fold + d, folds) * subs + of_sub) * span + k * step
+        return ext.at[pl.ds(first, step), pl.ds(half * TZ, TZ), :]
+
+    def rows(k):
+        return pl.ds(k * step, step)
+
+    order = list(range(1, folds)) + [0]
+    to_sub = {}
+    for group in (order[:-1], order[-1:]):
+        for half in (1, 0):
+            for d in group:
+                for k in range(chunks):
+                    for e in range(1, subs):
+                        peer = lax.rem(sub + e, subs)
+                        copy = pltpu.make_async_remote_copy(
+                            src_ref=own(d, peer, half, k),
+                            dst_ref=got_sub.at[e - 1, d, half, rows(k)],
+                            send_sem=sub_send.at[e - 1, d, half, k],
+                            recv_sem=sub_recv.at[e - 1, d, half, k],
+                            device_id={"sub": peer},
+                            device_id_type=mesh_id,
+                        )
+                        copy.start()
+                        to_sub[e, d, half, k] = copy
+
+    def chip_sum(d, half, k):
+        total = own(d, sub, half, k)[...].astype(f32)
+        for e in range(1, subs):
+            to_sub[e, d, half, k].wait_recv()
+            total = total + got_sub[e - 1, d, half, rows(k)].astype(f32)
+        return total
+
+    to_fold = {}
+    for half in (1, 0):
+        for d in range(1, folds):
+            for k in range(chunks):
+                part[d - 1, half, rows(k)] = chip_sum(d, half, k).astype(bf16)
+                copy = pltpu.make_async_remote_copy(
+                    src_ref=part.at[d - 1, half, rows(k)],
+                    dst_ref=got_fold.at[d - 1, half, rows(k)],
+                    send_sem=fold_send.at[d - 1, half, k],
+                    recv_sem=fold_recv.at[d - 1, half, k],
+                    device_id={"folds": lax.rem(fold + d, folds)},
+                    device_id_type=mesh_id,
+                )
+                copy.start()
+                to_fold[d, half, k] = copy
+
+    def full_sum(half, k):
+        total = chip_sum(0, half, k)
+        for d in range(1, folds):
+            to_fold[d, half, k].wait_recv()
+            total = total + got_fold[d - 1, half, rows(k)].astype(f32)
+        return total
+
+    to_tile = [
+        pltpu.make_async_remote_copy(
+            src_ref=tail.at[rows(k)],
+            dst_ref=got_tail.at[rows(k)],
+            send_sem=tile_send.at[k],
+            recv_sem=tile_recv.at[k],
+            device_id={"tiles": lax.rem(tile + 1, tiles)},
+            device_id_type=mesh_id,
+        )
+        for k in range(chunks)
+    ]
+    for k in range(chunks):
+        tail[rows(k)] = full_sum(1, k).astype(bf16)
+
+        @pl.when(tile < tiles - 1)
+        def _():
+            to_tile[k].start()
+
+    for k in range(chunks):
+        out[rows(k)] = full_sum(0, k)
+
+    @pl.when(tile > 0)
+    def _():
+        for k in range(chunks):
+            to_tile[k].wait_recv()
+            out[rows(k)] += got_tail[rows(k)].astype(f32)
+
+    for copy in list(to_sub.values()) + list(to_fold.values()):
+        copy.wait_send()
+
+    @pl.when(tile < tiles - 1)
+    def _():
+        for copy in to_tile:
+            copy.wait_send()
+
+
+def exchange(ext):
+    folds, subs = lax.axis_size("folds"), lax.axis_size("sub")
+    span = VX // (folds * subs)
+    lanes = VY * CLASSES
+    chunks = 2 if span % 2 == 0 else 1
+    vmem = pl.BlockSpec(memory_space=pltpu.VMEM)
+    dma = pltpu.SemaphoreType.DMA
+    return pl.pallas_call(
+        exchange_kernel,
+        out_shape=jax.ShapeDtypeStruct((span, TZ, lanes), f32),
+        in_specs=[vmem],
+        out_specs=vmem,
+        scratch_shapes=[
+            pltpu.VMEM((subs - 1, folds, 2, span, TZ, lanes), bf16),
+            pltpu.VMEM((folds - 1, 2, span, TZ, lanes), bf16),
+            pltpu.VMEM((folds - 1, 2, span, TZ, lanes), bf16),
+            pltpu.VMEM((span, TZ, lanes), bf16),
+            pltpu.VMEM((span, TZ, lanes), bf16),
+            dma((subs - 1, folds, 2, chunks)),
+            dma((subs - 1, folds, 2, chunks)),
+            dma((folds - 1, 2, chunks)),
+            dma((folds - 1, 2, chunks)),
+            dma((chunks,)),
+            dma((chunks,)),
+        ],
+        compiler_params=pltpu.CompilerParams(
+            collective_id=0, has_side_effects=True, vmem_limit_bytes=32 * 1024 * 1024
+        ),
+    )(ext)
+
+
 def on_device(
     features,
     conv_first,
@@ -266,12 +439,7 @@
         corners,
         counts,
     )
-    shares = lax.psum_scatter(extended, ("folds", "sub"), scatter_dimension=0, tiled=True)
-    length = lax.axis_size("tiles")
-    pairs = [(i, i + 1) for i in range(length - 1)]
-    arrived = lax.ppermute(shares[:, TZ:], "tiles", pairs)
-    total = shares[:, :TZ].astype(f32) + arrived.astype(f32)
-    return total.transpose(1, 0, 2)
+    return exchange(extended).transpose(1, 0, 2)
 
 
 def solution(mesh):

time: 72.3 us -> 34.8 us (0.48)
  waiting for transfers between devices: 35.4 us -> 0 us
  Pallas kernels: 12.5 us -> 27.8 us
  between operations: 13.4 us -> 0.03 us
  starting transfers between devices: 3.43 us -> 0 us
  other arithmetic: 1.74 us -> 0 us
  local copies, waits for them, and re-layouts: 5.54 us -> 6.79 us
    reduce_scatter x1 -> x0, waiting for transfers between devices: 31.2 us -> none  [on_device(): lax.psum_scatter(extended, ('folds', 'sub'), scatter_dimension=0, tiled=T...]
    pallas_call x0 -> x1, Pallas kernels: none -> 15.2 us  [exchange(): pl.pallas_call(exchange_kernel, out_shape=jax.ShapeDtypeStruct((span, TZ,...]
    ppermute x1 -> x0, waiting for transfers between devices: 4.13 us -> none  [on_device(): arrived = lax.ppermute(shares[:, TZ:], 'tiles', pairs)]
    ppermute x1 -> x0, starting transfers between devices: 3.42 us -> none  [on_device(): arrived = lax.ppermute(shares[:, TZ:], 'tiles', pairs)]
    unnamed x3 -> x6, local copies, waits for them, and re-layouts: 4.59 us -> 6.79 us
    transpose x1 -> x0, other arithmetic: 1.74 us -> none  [on_device(): return total.transpose(1, 0, 2)]
    slice x1 -> x0, local copies, waits for them, and re-layouts: 0.95 us -> none  [on_device(): arrived = lax.ppermute(shares[:, TZ:], 'tiles', pairs)]
  transfers between devices with their start and end apart: 2 -> 0, of which waited for: 2 -> 0; matrix products, arithmetic and copies ran while one was open for 0% -> 0% of each run, Pallas kernels for 0% -> 0%
where the time goes in v1:
time: 34.8 us; the launch traced here: 34.6 us
  Pallas kernels  27.8 us (80%)
  local copies, waits for them, and re-layouts  6.79 us (20%)
    pallas_call x1, Pallas kernels, exchange(): pl.pallas_call(exchange_kernel, out_shape=jax.ShapeDtypeStruct((span, TZ,...  15.2 us
    pallas_call x1, Pallas kernels, decode(): pl.pallas_call(decode_kernel, out_shape=jax.ShapeDtypeStruct((VX, EXT, VY...  12.5 us
    unnamed x6, local copies, waits for them, and re-layouts  6.79 us

profile of v1, /device:TPU:0, one launch (start us, length us, event | category | flops | bytes accessed | tf_op | source)
XLA Modules:
  0.0 34.6 jit_solution(2752302367713354633)
XLA Ops:
  0.0 1.4 %copy.14.counts = s32[4,2]{1,0:T(4,128)} copy(s32[4,2]{0,1:T(2,128)} %param.21) | data formatting | bytes 64 | tf_op args[10]
  1.4 1.4 %copy.13 = bf16[1,32,16]{2,1,0:T(8,128)(2,1)} copy(bf16[1,32,16]{1,2,0:T(8,128)(2,1)} %param.18) | data formatting | bytes 2048 | tf_op args[7]
  2.7 1.9 %copy.12 = bf16[1,3,3,3,64,32]{5,4,3,2,1,0:T(8,128)(2,1)} copy(bf16[1,3,3,3,64,32]{4,5,3,2,1,0:T(8,128)(2,1)} %param.12) | data formatting | bytes 221184 | tf_op args[1]
  4.6 12.5 %shard_map.109.ext = bf16[40,32,640]{2,1,0:T(8,128)(2,1)} custom-call(bf16[2,256,1024]{2,1,0:T(8,128)(2,1)} %bitcast.7, bf16[1728,32]{1,0:T(8,128)(2,1)} %bitcast.6, f32[1,32]{1,0:T(1,128)} %gain_first.1, f32[1,32]{1,0:T(1,128)} %shift_first.1, bf16[864,32]{1,0:T(8,128)(2,1)} %bitcast.8, f32[1,32]{1,0:T(1,128)} %gain_second.1, f32[1,32]{1,0:T(1,128)} %shift_second.1, ...), custom_call_target="tpu_custom_call" | custom-call | tf_op jit(solution)/shard_map/pallas_call | solution.py:213
  17.2 0.0 copy-start
  17.2 1.4 %copy-done = bf16[40,32,640]{2,1,0:T(8,128)(2,1)S(1)} copy-done((bf16[40,32,640]{2,1,0:T(8,128)(2,1)S(1)}, bf16[40,32,640]{2,1,0:T(8,128)(2,1)}, u32[]{:S(2)}) %copy-start) | copy-done | bytes 1638424
  18.6 15.2 %shard_map.110 = f32[10,16,640]{2,1,0:T(8,128)S(1)} custom-call(bf16[40,32,640]{2,1,0:T(8,128)(2,1)S(1)} %copy-done), custom_call_target="tpu_custom_call" | custom-call | tf_op jit(solution)/shard_map/pallas_call | solution.py:392
  33.8 0.8 %copy.16 = f32[16,10,640]{2,0,1:T(8,128)} copy(f32[16,10,640]{2,0,1:T(8,128)S(1)} %bitcast.5) | data formatting | bytes 819200
Async XLA Ops:
  17.2 1.4 %copy-start = (bf16[40,32,640]{2,1,0:T(8,128)(2,1)S(1)}, bf16[40,32,640]{2,1,0:T(8,128)(2,1)}, u32[]{:S(2)}) copy-start(bf16[40,32,640]{2,1,0:T(8,128)(2,1)} %shard_map.109.ext) | copy-start | bytes 4915204

commit v2 on v1

--- a/solution.py
+++ b/solution.py
@@ -42,17 +42,21 @@
     return exact_dot(vec, pick)
 
 
-def build_band(taps_ref, band, in_width, lead):
+def build_band(taps_ref, band, in_width, lead, flipped):
     pick = one_hot(iota((CH, 8 * CH), 0) == iota((CH, 8 * CH), 1) % CH).astype(bf16)
-    band[...] = jnp.zeros_like(band)
+    written = ((lead - 1) * in_width, (lead + 9) * in_width)
+    for lo, hi in ((0, written[0]), (written[1], band.shape[1])):
+        band[:, lo:hi, :] = jnp.zeros((3, hi - lo, band.shape[2]), bf16)
     out_voxel = iota((in_width, 8 * CH), 1) // CH
     for dz in range(3):
         for dx in range(3):
-            start = (dz * 3 + dx) * 3 * in_width
+            start = (dz * 3 + dx) * 3
+            rows = CH if flipped else in_width
             spread = [
-                jnp.dot(
-                    taps_ref[start + dy * in_width : start + (dy + 1) * in_width, :],
+                lax.dot_general(
+                    taps_ref[(start + dy) * rows : (start + dy + 1) * rows, :],
                     pick,
+                    (((0 if flipped else 1,), (0,)), ((), ())),
                     preferred_element_type=f32,
                 )
                 for dy in range(3)
@@ -148,25 +152,27 @@
         normed[w, :WE, :] = jnp.zeros((WE, normed.shape[2]), bf16)
         normed[w, WE + ROWS :, :] = jnp.zeros((WE, normed.shape[2]), bf16)
     ext[...] = jnp.zeros_like(ext)
-    build_band(taps_first, band_first, cin, 4)
-    build_band(taps_second, band_second, CH, 8)
+    build_band(taps_first, band_first, cin, 2, True)
+    build_band(taps_second, band_second, CH, 4, False)
     gains = [spread_lanes(g[...], WE * CH) for g in (gain_first, gain_second)]
     shifts = [spread_lanes(s[...], WE * CH) for s in (shift_first, shift_second)]
     for load in loads:
         load.wait()
-    convolve(padded, band_first, hidden, ((0, 12 * cin), (4 * cin, 12 * cin)), (4 * cin, 0))
+    convolve(padded, band_first, hidden, ((0, 10 * cin), (6 * cin, 10 * cin)), (2 * cin, 0))
     for w in range(n):
         normed[w, WE : WE + ROWS, :] = normalize(
             hidden[w * ROWS : (w + 1) * ROWS, :], gains[0], shifts[0]
         )
-    convolve(normed, band_second, hidden, ((0, 16 * CH), (0, 16 * CH)), (8 * CH, 0))
+    convolve(normed, band_second, hidden, ((0, 12 * CH), (4 * CH, 12 * CH)), (4 * CH, 0))
 
     tile = lax.axis_index("tiles")
-    live_count = counts[tile, lax.axis_index("sub")]
+    live_count = counts[lax.axis_index("sub"), tile]
     width = WE * CH
     pick_rows = one_hot(iota((width, CH), 0) % CH == iota((width, CH), 1)).astype(bf16)
     pick_lanes = one_hot(iota((CLASSES, LANES), 0) == iota((CLASSES, LANES), 1) % CLASSES)
-    head_rows = jnp.dot(pick_rows, head_weight[...], preferred_element_type=f32).astype(bf16)
+    head_rows = lax.dot_general(
+        pick_rows, head_weight[...], (((1,), (1,)), ((), ())), preferred_element_type=f32
+    ).astype(bf16)
     head_full = jnp.dot(head_rows, pick_lanes.astype(bf16), preferred_element_type=f32)
     bias = spread_lanes(head_bias[...], LANES)
     head_gap = iota((width, LANES), 1) // CLASSES - iota((width, LANES), 0) // CH
@@ -213,30 +219,30 @@
     return pl.pallas_call(
         decode_kernel,
         out_shape=jax.ShapeDtypeStruct((VX, EXT, VY * CLASSES), bf16),
-        in_specs=[pl.BlockSpec(memory_space=pl.ANY)] + [vmem] * 8 + [smem] * 2,
+        in_specs=[pl.BlockSpec(memory_space=pltpu.HBM)] + [vmem] * 8 + [smem] * 2,
         out_specs=vmem,
         scratch_shapes=[
             pltpu.VMEM((n, ROWS + 2 * WE, in_width), bf16),
             pltpu.VMEM((n, ROWS + 2 * WE, WE * CH), bf16),
-            pltpu.VMEM((3, 16 * cin, 24 * CH), bf16),
-            pltpu.VMEM((3, 24 * CH, 24 * CH), bf16),
+            pltpu.VMEM((3, 12 * cin, 24 * CH), bf16),
+            pltpu.VMEM((3, 16 * CH, 24 * CH), bf16),
             pltpu.VMEM((n * ROWS, WE * CH), f32),
             pltpu.VMEM((VX, EXT, VY * CLASSES), f32),
             pltpu.SemaphoreType.DMA((n,)),
         ],
-        compiler_params=pltpu.CompilerParams(vmem_limit_bytes=56 * 1024 * 1024),
+        compiler_params=pltpu.CompilerParams(vmem_limit_bytes=28 * 1024 * 1024),
     )(
         features.reshape(n, ROWS, in_width),
-        taps_first.reshape(27 * cin, CH),
+        taps_first.swapaxes(-1, -2).reshape(27 * CH, cin),
         gf,
         sf,
         taps_second.reshape(27 * CH, CH),
         gs,
         ss,
-        hw,
+        hw.T,
         hb,
         corners,
-        counts,
+        counts.T,
     )
 
 
@@ -408,7 +414,7 @@
             dma((chunks,)),
         ],
         compiler_params=pltpu.CompilerParams(
-            collective_id=0, has_side_effects=True, vmem_limit_bytes=32 * 1024 * 1024
+            collective_id=0, has_side_effects=True, vmem_limit_bytes=12 * 1024 * 1024
         ),
     )(ext)
 

time: 34.8 us -> 35.1 us (level)
  local copies, waits for them, and re-layouts: 6.79 us -> 9.17 us
  Pallas kernels: 27.8 us -> 25.6 us
    unnamed x6 -> x23, local copies, waits for them, and re-layouts: 6.79 us -> 9.17 us
    pallas_call x1, Pallas kernels: 12.5 us -> 10.3 us  [decode(): pl.pallas_call(decode_kernel, out_shape=jax.ShapeDtypeStruct((VX, EXT, VY...]
where the time goes in v2:
time: 35.1 us; the launch traced here: 34.8 us
  Pallas kernels  25.6 us (73%)
  local copies, waits for them, and re-layouts  9.17 us (26%)
    pallas_call x1, Pallas kernels, exchange(): pl.pallas_call(exchange_kernel, out_shape=jax.ShapeDtypeStruct((span, TZ,...  15.3 us
    pallas_call x1, Pallas kernels, decode(): pl.pallas_call(decode_kernel, out_shape=jax.ShapeDtypeStruct((VX, EXT, VY...  10.3 us
    unnamed x23, local copies, waits for them, and re-layouts  9.17 us

profile of v2, /device:TPU:0, one launch (start us, length us, event | category | flops | bytes accessed | tf_op | source)
XLA Modules:
  0.0 34.8 jit_solution(3465973279658150114)
XLA Ops:
  0.0 0.0 copy-start
  0.0 1.2 %copy-done = bf16[1,2,16,16,1024]{4,3,2,1,0:T(8,128)(2,1)S(1)} copy-done((bf16[1,2,16,16,1024]{4,3,2,1,0:T(8,128)(2,1)S(1)}, bf16[1,2,16,16,1024]{4,3,2,1,0:T(8,128)(2,1)}, u32[]{:S(2)}) %copy-start) | copy-done | bytes 1048600
  1.2 0.0 copy-start.1
  1.2 0.9 %copy-done.1 = bf16[1,3,3,3,64,32]{4,5,3,2,1,0:T(8,128)(2,1)S(1)} copy-done((bf16[1,3,3,3,64,32]{4,5,3,2,1,0:T(8,128)(2,1)S(1)}, bf16[1,3,3,3,64,32]{4,5,3,2,1,0:T(8,128)(2,1)}, u32[]{:S(2)}) %copy-start.1) | copy-done | bytes 110616
  2.2 0.0 copy-start.2
  2.2 0.9 %copy-done.2 = bf16[1,3,3,3,32,32]{5,4,3,2,1,0:T(8,128)(2,1)S(1)} copy-done((bf16[1,3,3,3,32,32]{5,4,3,2,1,0:T(8,128)(2,1)S(1)}, bf16[1,3,3,3,32,32]{5,4,3,2,1,0:T(8,128)(2,1)}, u32[]{:S(2)}) %copy-start.2) | copy-done | bytes 55320
  3.1 0.0 copy-start.3
  3.1 0.7 %copy-done.3 = bf16[1,32,16]{1,2,0:T(8,128)(2,1)S(1)} copy-done((bf16[1,32,16]{1,2,0:T(8,128)(2,1)S(1)}, bf16[1,32,16]{1,2,0:T(8,128)(2,1)}, u32[]{:S(2)}) %copy-start.3) | copy-done | bytes 1048
  3.8 0.0 copy-start.4
  3.8 0.7 %copy-done.4 = s32[2,3]{1,0:T(2,128)S(1)} copy-done((s32[2,3]{1,0:T(2,128)S(1)}, s32[2,3]{1,0:T(2,128)}, u32[]{:S(2)}) %copy-start.4) | copy-done | bytes 48
  4.5 0.0 copy-start.5
  4.5 0.7 %copy-done.5 = s32[4,2]{0,1:T(2,128)S(1)} copy-done((s32[4,2]{0,1:T(2,128)S(1)}, s32[4,2]{0,1:T(2,128)}, u32[]{:S(2)}) %copy-start.5) | copy-done | bytes 56
  5.1 0.0 copy-start.6
  5.1 0.7 %copy-done.6 = f32[1,32]{1,0:T(1,128)S(1)} copy-done((f32[1,32]{1,0:T(1,128)S(1)}, f32[1,32]{1,0:T(1,128)}, u32[]{:S(2)}) %copy-start.6) | copy-done | bytes 152
  5.8 0.0 copy-start.7
  5.8 0.7 %copy-done.7 = f32[1,32]{1,0:T(1,128)S(1)} copy-done((f32[1,32]{1,0:T(1,128)S(1)}, f32[1,32]{1,0:T(1,128)}, u32[]{:S(2)}) %copy-start.7) | copy-done | bytes 152
  6.5 0.0 copy-start.8
  6.5 0.7 %copy-done.8 = f32[1,32]{1,0:T(1,128)S(1)} copy-done((f32[1,32]{1,0:T(1,128)S(1)}, f32[1,32]{1,0:T(1,128)}, u32[]{:S(2)}) %copy-start.8) | copy-done | bytes 152
  7.1 0.0 copy-start.9
  7.1 0.7 %copy-done.9 = f32[1,32]{1,0:T(1,128)S(1)} copy-done((f32[1,32]{1,0:T(1,128)S(1)}, f32[1,32]{1,0:T(1,128)}, u32[]{:S(2)}) %copy-start.9) | copy-done | bytes 152
  7.8 0.0 copy-start.10
  7.8 0.7 %copy-done.10 = f32[1,16]{1,0:T(1,128)S(1)} copy-done((f32[1,16]{1,0:T(1,128)S(1)}, f32[1,16]{1,0:T(1,128)}, u32[]{:S(2)}) %copy-start.10) | copy-done | bytes 88
  8.4 10.3 %shard_map.109.ext = bf16[40,32,640]{2,1,0:T(8,128)(2,1)S(1)} custom-call(bf16[2,256,1024]{2,1,0:T(8,128)(2,1)S(1)} %bitcast.13, bf16[864,64]{1,0:T(8,128)(2,1)S(1)} %bitcast.14, f32[1,32]{1,0:T(1,128)S(1)} %copy-done.6, f32[1,32]{1,0:T(1,128)S(1)} %copy-done.7, bf16[864,32]{1,0:T(8,128)(2,1)S(1)} %bitcast.15, f32[1,32]{1,0:T(1,128)S(1)} %copy-done.8, ...), custom_call_target="tpu_custom_call" | custom-call | tf_op jit(solution)/shard_map/pallas_call | solution.py:219
  18.7 15.3 %shard_map.110 = f32[10,16,640]{2,1,0:T(8,128)S(1)} custom-call(bf16[40,32,640]{2,1,0:T(8,128)(2,1)S(1)} %shard_map.109.ext), custom_call_target="tpu_custom_call" | custom-call | tf_op jit(solution)/shard_map/pallas_call | solution.py:398
  34.0 0.8 %copy.13 = f32[16,10,640]{2,0,1:T(8,128)} copy(f32[16,10,640]{2,0,1:T(8,128)S(1)} %bitcast.12) | data formatting | bytes 819200
Async XLA Ops:
  0.0 1.2 %copy-start = (bf16[1,2,16,16,1024]{4,3,2,1,0:T(8,128)(2,1)S(1)}, bf16[1,2,16,16,1024]{4,3,2,1,0:T(8,128)(2,1)}, u32[]{:S(2)}) copy-start(bf16[1,2,16,16,1024]{4,3,2,1,0:T(8,128)(2,1)} %param.11) | copy-start | bytes 3145732
  1.2 0.9 %copy-start.1 = (bf16[1,3,3,3,64,32]{4,5,3,2,1,0:T(8,128)(2,1)S(1)}, bf16[1,3,3,3,64,32]{4,5,3,2,1,0:T(8,128)(2,1)}, u32[]{:S(2)}) copy-start(bf16[1,3,3,3,64,32]{4,5,3,2,1,0:T(8,128)(2,1)} %param.12) | copy-start | bytes 331780
  2.2 0.9 %copy-start.2 = (bf16[1,3,3,3,32,32]{5,4,3,2,1,0:T(8,128)(2,1)S(1)}, bf16[1,3,3,3,32,32]{5,4,3,2,1,0:T(8,128)(2,1)}, u32[]{:S(2)}) copy-start(bf16[1,3,3,3,32,32]{5,4,3,2,1,0:T(8,128)(2,1)} %param.15) | copy-start | bytes 165892
  3.1 0.7 %copy-start.3 = (bf16[1,32,16]{1,2,0:T(8,128)(2,1)S(1)}, bf16[1,32,16]{1,2,0:T(8,128)(2,1)}, u32[]{:S(2)}) copy-start(bf16[1,32,16]{1,2,0:T(8,128)(2,1)} %param.18) | copy-start | bytes 3076
  3.8 0.7 %copy-start.4 = (s32[2,3]{1,0:T(2,128)S(1)}, s32[2,3]{1,0:T(2,128)}, u32[]{:S(2)}) copy-start(s32[2,3]{1,0:T(2,128)} %corners.1) | copy-start | bytes 76
  4.5 0.7 %copy-start.5 = (s32[4,2]{0,1:T(2,128)S(1)}, s32[4,2]{0,1:T(2,128)}, u32[]{:S(2)}) copy-start(s32[4,2]{0,1:T(2,128)} %param.21) | copy-start | bytes 100
  5.1 0.7 %copy-start.6 = (f32[1,32]{1,0:T(1,128)S(1)}, f32[1,32]{1,0:T(1,128)}, u32[]{:S(2)}) copy-start(f32[1,32]{1,0:T(1,128)} %gain_first.1) | copy-start | bytes 388
  5.8 0.7 %copy-start.7 = (f32[1,32]{1,0:T(1,128)S(1)}, f32[1,32]{1,0:T(1,128)}, u32[]{:S(2)}) copy-start(f32[1,32]{1,0:T(1,128)} %shift_first.1) | copy-start | bytes 388
  6.5 0.7 %copy-start.8 = (f32[1,32]{1,0:T(1,128)S(1)}, f32[1,32]{1,0:T(1,128)}, u32[]{:S(2)}) copy-start(f32[1,32]{1,0:T(1,128)} %gain_second.1) | copy-start | bytes 388
  7.1 0.7 %copy-start.9 = (f32[1,32]{1,0:T(1,128)S(1)}, f32[1,32]{1,0:T(1,128)}, u32[]{:S(2)}) copy-start(f32[1,32]{1,0:T(1,128)} %shift_second.1) | copy-start | bytes 388
  7.8 0.7 %copy-start.10 = (f32[1,16]{1,0:T(1,128)S(1)}, f32[1,16]{1,0:T(1,128)}, u32[]{:S(2)}) copy-start(f32[1,16]{1,0:T(1,128)} %head_bias.1) | copy-start | bytes 196

commit v3 on v2

--- a/solution.py
+++ b/solution.py
@@ -230,7 +230,7 @@
             pltpu.VMEM((VX, EXT, VY * CLASSES), f32),
             pltpu.SemaphoreType.DMA((n,)),
         ],
-        compiler_params=pltpu.CompilerParams(vmem_limit_bytes=28 * 1024 * 1024),
+        compiler_params=pltpu.CompilerParams(vmem_limit_bytes=60 * 1024 * 1024),
     )(
         features.reshape(n, ROWS, in_width),
         taps_first.swapaxes(-1, -2).reshape(27 * CH, cin),

time: 35.1 us -> 29.5 us (0.84)
  local copies, waits for them, and re-layouts: 9.17 us -> 2.18 us
  Pallas kernels: 25.6 us -> 27.2 us
    unnamed x23 -> x3, local copies, waits for them, and re-layouts: 9.17 us -> 2.18 us
    pallas_call x1, Pallas kernels: 10.3 us -> 11.9 us  [decode(): pl.pallas_call(decode_kernel, out_shape=jax.ShapeDtypeStruct((VX, EXT, VY...]
where the time goes in v3:
time: 29.5 us; the launch traced here: 29.4 us
  Pallas kernels  27.2 us (92%)
  local copies, waits for them, and re-layouts  2.18 us (7%)
    pallas_call x1, Pallas kernels, exchange(): pl.pallas_call(exchange_kernel, out_shape=jax.ShapeDtypeStruct((span, TZ,...  15.3 us
    pallas_call x1, Pallas kernels, decode(): pl.pallas_call(decode_kernel, out_shape=jax.ShapeDtypeStruct((VX, EXT, VY...  11.9 us
    unnamed x3, local copies, waits for them, and re-layouts  2.18 us

profile of v3, /device:TPU:0, one launch (start us, length us, event | category | flops | bytes accessed | tf_op | source)
XLA Modules:
  0.0 29.4 jit_solution(8287793046381510299)
XLA Ops:
  0.0 11.9 %shard_map.109.ext = bf16[40,32,640]{2,1,0:T(8,128)(2,1)} custom-call(bf16[2,256,1024]{2,1,0:T(8,128)(2,1)} %bitcast.13, bf16[864,64]{1,0:T(8,128)(2,1)} %bitcast.14, f32[1,32]{1,0:T(1,128)} %gain_first.1, f32[1,32]{1,0:T(1,128)} %shift_first.1, bf16[864,32]{1,0:T(8,128)(2,1)} %bitcast.15, f32[1,32]{1,0:T(1,128)} %gain_second.1, f32[1,32]{1,0:T(1,128)} %shift_second.1, ...), custom_call_target="tpu_custom_call" | custom-call | tf_op jit(solution)/shard_map/pallas_call | solution.py:219
  11.9 0.0 copy-start
  11.9 1.4 %copy-done = bf16[40,32,640]{2,1,0:T(8,128)(2,1)S(1)} copy-done((bf16[40,32,640]{2,1,0:T(8,128)(2,1)S(1)}, bf16[40,32,640]{2,1,0:T(8,128)(2,1)}, u32[]{:S(2)}) %copy-start) | copy-done | bytes 1638424
  13.3 15.3 %shard_map.110 = f32[10,16,640]{2,1,0:T(8,128)S(1)} custom-call(bf16[40,32,640]{2,1,0:T(8,128)(2,1)S(1)} %copy-done), custom_call_target="tpu_custom_call" | custom-call | tf_op jit(solution)/shard_map/pallas_call | solution.py:398
  28.6 0.8 %copy.13 = f32[16,10,640]{2,0,1:T(8,128)} copy(f32[16,10,640]{2,0,1:T(8,128)S(1)} %bitcast.12) | data formatting | bytes 819200
Async XLA Ops:
  11.9 1.4 %copy-start = (bf16[40,32,640]{2,1,0:T(8,128)(2,1)S(1)}, bf16[40,32,640]{2,1,0:T(8,128)(2,1)}, u32[]{:S(2)}) copy-start(bf16[40,32,640]{2,1,0:T(8,128)(2,1)} %shard_map.109.ext) | copy-start | bytes 4915204
